TPU v7x, 32 devices: a whole 2x2x4 slice. The times are simulated.
32 devices in a mesh: expert: 8 (over z, y), replica: 4 (over x, core).
Axes of the slice: x: 2, y: 2, z: 4, core: 2. Of those that a mesh axis runs over, the one named last changes fastest.
Arguments:
- tokens: bfloat16 [4096, 2048], P(('expert', 'replica')), may hold values from -6 to 6
- expert_ids: int32 [4096, 8], P(('expert', 'replica')), may hold values from 0 to 31, as said below
- gates: float32 [4096, 8], P(('expert', 'replica')), may hold values from 0.02 to 0.25
- cotangent: bfloat16 [4096, 2048], P(('expert', 'replica')), may hold values from -6 to 6
- expert_weights: bfloat16 [32, 2048, 1152], P(('expert', 'replica')), may hold values from -0.125 to 0.125
- moment_first: bfloat16 [32, 2048, 1152], P(('expert', 'replica')), may hold values from -0.00021362305 to 0.00021362305
- moment_second: bfloat16 [32, 2048, 1152], P(('expert', 'replica')), may hold values from 1.3242243e-09 to 1.3213139e-08
- hot_slot: int32 [8], P('expert'), may hold values from 0 to 3
Outputs:
- mixed: bfloat16 [4096, 2048], P(('expert', 'replica'))
- input_grad: bfloat16 [4096, 2048], P(('expert', 'replica'))
- gate_grad: float32 [4096, 8], P(('expert', 'replica'))
- new_weights: bfloat16 [32, 2048, 1152], P(('expert', 'replica'))
- hot_copy: bfloat16 [32, 2048, 1152], P(('expert', 'replica'))
Inputs may be any that keep to these rules, and one draw needn't show every extreme that they name: `expert_ids`: each token names 8 different experts. Experts form 8 groups of 4 consecutive numbers. Of the choices of the 128 tokens of one device (aligned blocks of rows), exactly 128 name experts of each group; in group a the expert a * 4 + hot_slot[a] is named exactly 64 times, every other expert at most 32 times, and one of them exactly 32 times.
All inputs are finite; a program needn't handle non-finite values.
Results may differ from a plain program's by a relative error of at most 0.011.
Values may be sent and summed in bfloat16 or wider, within the bound.
No kernel may reach another device: no remote copies, remote signals or barrier semaphores. Data moves between devices by JAX's collectives and lax.ppermute only.
A program may use at most 256 MiB of HBM per device.

v0:
```python
import jax
import jax.numpy as jnp
from jax import lax
from jax.sharding import PartitionSpec as P

beta_first = 0.9
beta_second = 0.95
adam_eps = 1e-08
rate = 0.05
clip_norm = 1.0
bias_first = 1.0 - 0.9**10
bias_second = 1.0 - 0.95**10


def broadcast(value, axis, source):
    kept = jnp.where(lax.axis_index(axis) == source, value, 0).astype(value.dtype)
    return lax.psum(kept, axis)


def expert_forward(row_block, weights, hidden_width):
    gate_up = jnp.dot(row_block, weights[:, : 2 * hidden_width], preferred_element_type=jnp.float32)
    gate_in = gate_up[:, :hidden_width]
    up_part = gate_up[:, hidden_width:]
    hidden = (gate_in * jax.nn.sigmoid(gate_in) * up_part).astype(jnp.bfloat16)
    outputs = lax.dot_general(
        hidden,
        weights[:, 2 * hidden_width :],
        (((1,), (1,)), ((), ())),
        preferred_element_type=jnp.float32,
    ).astype(jnp.bfloat16)
    return (outputs, gate_up, hidden)


def expert_backward(cot_block, gate_up, weights, hidden_width):
    gate_in = gate_up[:, :hidden_width]
    up_part = gate_up[:, hidden_width:]
    sigmoid_gate = jax.nn.sigmoid(gate_in)
    hidden_grad = jnp.dot(
        cot_block, weights[:, 2 * hidden_width :], preferred_element_type=jnp.float32
    )
    grad_gate = hidden_grad * up_part * sigmoid_gate * (1.0 + gate_in * (1.0 - sigmoid_gate))
    grad_up = hidden_grad * gate_in * sigmoid_gate
    input_both = jnp.concatenate([grad_gate, grad_up], axis=1).astype(jnp.bfloat16)
    slot_grads = lax.dot_general(
        input_both,
        weights[:, : 2 * hidden_width],
        (((1,), (1,)), ((), ())),
        preferred_element_type=jnp.float32,
    ).astype(jnp.bfloat16)
    return (slot_grads, input_both)


def partial_sums(row_block, cot_block, input_both, hidden, leading):
    in_part = jnp.einsum(
        "arcd,arcg->rdg",
        row_block.reshape(leading + (-1,)),
        input_both.reshape(leading + (-1,)),
        preferred_element_type=jnp.float32,
    )
    down_part = jnp.einsum(
        "arcd,arcf->rdf",
        cot_block.reshape(leading + (-1,)),
        hidden.reshape(leading + (-1,)),
        preferred_element_type=jnp.float32,
    )
    partial_value = lax.optimization_barrier(
        jnp.concatenate([in_part, down_part], axis=2).astype(jnp.bfloat16)
    )
    return jnp.sum(partial_value.astype(jnp.float32), axis=0)


def place_slots(target, bins, room, allowed):
    one_hot = (target[:, None] == jnp.arange(bins, dtype=jnp.int32)[None, :]).astype(
        jnp.int32
    ) * allowed[:, None].astype(jnp.int32)
    ahead = jnp.cumsum(one_hot, axis=0) - one_hot
    return target * room + jnp.sum(ahead * one_hot, axis=1)


def to_experts(row_block):
    return lax.all_to_all(row_block, ("expert", "replica"), split_axis=0, concat_axis=0, tiled=True)


def from_experts(row_block):
    return lax.all_to_all(row_block, ("expert", "replica"), split_axis=0, concat_axis=0, tiled=True)


def shards(
    tokens, expert_ids, gates, cotangent, expert_weights, moment_first, moment_second, hot_slot
):
    groups = lax.axis_size("expert")
    owners = lax.axis_size("replica")
    experts = groups * owners
    token_count, chosen = expert_ids.shape
    slot_total = token_count * chosen
    hidden_width = expert_weights.shape[2] // 3
    capacity = 2 * slot_total // experts
    weights = expert_weights[0]
    routed = expert_ids.reshape(-1)
    slot_numbers = jnp.arange(slot_total, dtype=jnp.int32)
    zero_half = jnp.zeros((), jnp.bfloat16)
    all_true = jnp.ones((slot_total,), jnp.bool_)
    hot_member = hot_slot[0]
    slot_place = place_slots(routed, experts, capacity, all_true)
    slot_source = jnp.zeros((experts * capacity,), jnp.int32).at[slot_place].set(slot_numbers)
    slot_filled = jnp.zeros((experts * capacity,), jnp.bool_).at[slot_place].set(True)
    arrived = to_experts(jnp.where(slot_filled[:, None], tokens[slot_source // chosen], zero_half))
    outputs, gate_up, hidden = expert_forward(arrived, weights, hidden_width)
    slot_out = from_experts(outputs)[slot_place]
    slot_wide = slot_out.astype(jnp.float32).reshape(token_count, chosen, -1)
    mixed = jnp.einsum("tk,tkd->td", gates, slot_wide).astype(jnp.bfloat16)
    gate_grad = jnp.einsum("td,tkd->tk", cotangent.astype(jnp.float32), slot_wide)
    slot_cot = (
        (gates[:, :, None] * cotangent[:, None, :].astype(jnp.float32))
        .astype(jnp.bfloat16)
        .reshape(slot_total, -1)
    )
    cot_arrived = to_experts(jnp.where(slot_filled[:, None], slot_cot[slot_source], zero_half))
    slot_grads, input_both = expert_backward(cot_arrived, gate_up, weights, hidden_width)
    gradient = partial_sums(arrived, cot_arrived, input_both, hidden, (groups, owners, capacity))
    slot_dx = from_experts(slot_grads)[slot_place]
    input_grad = jnp.sum(
        slot_dx.astype(jnp.float32).reshape(token_count, chosen, -1), axis=1
    ).astype(jnp.bfloat16)
    clip_bound = clip_norm * experts ** (-0.5)
    scale = jnp.minimum(1.0, clip_bound / (jnp.sqrt(jnp.sum(gradient * gradient)) + 1e-06))
    scaled = scale * gradient
    first = beta_first * moment_first[0].astype(jnp.float32) + (1.0 - beta_first) * scaled
    second = (
        beta_second * moment_second[0].astype(jnp.float32) + (1.0 - beta_second) * scaled * scaled
    )
    update = first / bias_first / (jnp.sqrt(second / bias_second) + adam_eps)
    new_weights = (weights.astype(jnp.float32) - rate * update).astype(jnp.bfloat16)
    hot_copy = broadcast(new_weights, "replica", hot_member)
    return (mixed, input_grad, gate_grad, new_weights[None], hot_copy[None])


def solution(mesh):
    return jax.shard_map(
        shards,
        mesh=mesh,
        in_specs=(
            P(("expert", "replica"), None),
            P(("expert", "replica"), None),
            P(("expert", "replica"), None),
            P(("expert", "replica"), None),
            P(("expert", "replica"), None, None),
            P(("expert", "replica"), None, None),
            P(("expert", "replica"), None, None),
            P("expert"),
        ),
        out_specs=(
            P(("expert", "replica"), None),
            P(("expert", "replica"), None),
            P(("expert", "replica"), None),
            P(("expert", "replica"), None, None),
            P(("expert", "replica"), None, None),
        ),
        check_vma=False,
    )
```

profile of v0, /device:TPU:0, one launch (start us, length us, event | category | flops | bytes accessed | tf_op | source)
XLA Modules:
  0.0 949.9 jit_solution(18028048421142596829)
XLA Ops:
  8.9 9.0 reduce-window.6
  31.9 19.1 %gather_fusion.2 = bf16[2048,2048]{1,0:T(8,128)(2,1)} fusion(bf16[1024,2048]{1,0:T(8,128)(2,1)} %fusion.19, s32[2048]{0:T(1024)S(1)} %get-tuple-element.13), kind=kCustom, calls=%fused_computation.2 | custom fusion | bytes 16785408 | tf_op jit(solution)/shard_map/gather | solution.py:118
  51.0 11.0 %gather_fusion = bf16[2048,2048]{1,0:T(8,128)(2,1)} fusion(bf16[128,2048]{1,0:T(8,128)(2,1)S(1)} %copy-done, s32[2048]{0:T(1024)S(1)} %get-tuple-element.14), kind=kCustom, calls=%fused_computation | custom fusion | bytes 16785408 | tf_op jit(solution)/shard_map/gather | solution.py:107
  62.0 9.2 broadcast_select_fusion
  71.2 190.7 %all_to_all.42 = bf16[32,64,2048]{2,1,0:T(8,128)(2,1)} all-to-all(bf16[32,64,2048]{2,1,0:T(8,128)(2,1)S(1)} %get-tuple-element.16), channel_id=1, replica_groups=mesh['expert'=8,'replica'=4] {'expert','replica'}, dimensions={0} | all-to-all | bytes 16777216 | tf_op jit(solution)/shard_map/all_to_all | solution.py:81
  272.8 11.8 %fusion.31 = f32[2048,768]{1,0:T(8,128)} fusion(bf16[2048,2048]{1,0:T(8,128)(2,1)} %bitcast.101, bf16[2048,1152]{0,1:T(8,128)(2,1)} %bitcast.94), kind=kOutput, calls=%fused_computation.59 | convolution fusion | flops 6442450944 | bytes 17825792 | tf_op jit(solution)/shard_map/dot_general | solution.py:21
  284.6 167.6 %all-to-all-done.2 = bf16[32,64,2048]{2,1,0:T(8,128)(2,1)} async-done(((bf16[32,64,2048]{2,1,0:T(8,128)(2,1)}), bf16[32,64,2048]{2,1,0:T(8,128)(2,1)}, u32[]{:S(2)}, u32[]{:S(2)}) %all-to-all-start.2) | async-done | bytes 8388640 | tf_op jit(solution)/shard_map/all_to_all | solution.py:81
  452.2 12.8 %multiply_convert_fusion.1 = (bf16[2048,384]{1,0:T(8,128)(2,1)S(1)}, bf16[2048,384]{1,0:T(8,128)(2,1)S(1)}, bf16[2048,384]{1,0:T(8,128)(2,1)}) fusion(f32[2048,768]{1,0:T(8,128)} %fusion.31, bf16[2048,2048]{1,0:T(8,128)(2,1)} %bitcast.14, bf16[2048,1152]{0,1:T(8,128)(2,1)} %bitcast.95), kind=kOutput, calls=%fused_computation.55 | convolution fusion | flops 3233808384 | bytes 20971520 | tf_op jit(solution)/shard_map/dot_general | solution.py:38
  465.0 9.0 convolution_convert_fusion
  474.0 14.4 %all-to-all-start.3 = ((bf16[32,64,2048]{2,1,0:T(8,128)(2,1)}), bf16[32,64,2048]{2,1,0:T(8,128)(2,1)}, u32[]{:S(2)}, u32[]{:S(2)}) async-start(bf16[32,64,2048]{2,1,0:T(8,128)(2,1)} %bitcast.103), calls=%async_computation.3 | async-start | bytes 16777216 | tf_op jit(solution)/shard_map/all_to_all | solution.py:85
  488.4 9.8 %convolution_convert_fusion.1 = bf16[2048,2048]{1,0:T(8,128)(2,1)} fusion(bf16[2048,384]{1,0:T(8,128)(2,1)} %get-tuple-element.12, bf16[2048,1152]{0,1:T(8,128)(2,1)} %bitcast.96), kind=kOutput, calls=%fused_computation.41 | convolution fusion | flops 3225419776 | bytes 11534336 | tf_op jit(solution)/shard_map/dot_general | solution.py:25
  498.1 176.3 %all-to-all-done.3 = bf16[32,64,2048]{2,1,0:T(8,128)(2,1)} async-done(((bf16[32,64,2048]{2,1,0:T(8,128)(2,1)}), bf16[32,64,2048]{2,1,0:T(8,128)(2,1)}, u32[]{:S(2)}, u32[]{:S(2)}) %all-to-all-start.3) | async-done | bytes 8388640 | tf_op jit(solution)/shard_map/all_to_all | solution.py:85
  678.2 6.7 copy.35
  692.4 9.9 %bitcast_convert_fusion.1 = bf16[4,2048,384]{1,2,0:T(8,128)(2,1)} fusion(bf16[8,4,64,2048]{3,2,1,0:T(8,128)(2,1)} %bitcast.24, bf16[8,4,64,384]{3,2,1,0:T(8,128)(2,1)} %bitcast.116), kind=kOutput, calls=%fused_computation.11 | convolution fusion | flops 3224371200 | bytes 16252928 | tf_op jit(solution)/shard_map/arcd,arcf->rdf/dot_general | solution.py:60
  702.3 12.4 %bitcast_convert_fusion = bf16[4,2048,768]{1,2,0:T(8,128)(2,1)} fusion(bf16[8,4,64,2048]{3,2,1,0:T(8,128)(2,1)} %bitcast.102, bf16[8,4,64,384]{3,2,1,0:T(8,128)(2,1)} %bitcast.115, bf16[8,4,64,384]{3,2,1,0:T(8,128)(2,1)S(1)} %bitcast.114), kind=kOutput, calls=%fused_computation.7 | convolution fusion | flops 6455033856 | bytes 24117248 | tf_op jit(solution)/shard_map/arcd,arcg->rdg/dot_general | solution.py:54
  714.7 20.3 %pad_maximum_fusion = bf16[4,2048,1152]{1,2,0:T(8,128)(2,1)} fusion(bf16[4,2048,384]{1,2,0:T(8,128)(2,1)} %bitcast_convert_fusion.1, bf16[4,2048,768]{1,2,0:T(8,128)(2,1)} %bitcast_convert_fusion), kind=kLoop, calls=%fused_computation.8 | loop fusion | flops 37748736 | bytes 37748736 | tf_op jit(solution)/shard_map/concatenate | solution.py:67
  735.0 14.7 %convert_reduce_fusion = f32[2048,1152]{0,1:T(8,128)} fusion(bf16[4,2048,1152]{1,2,0:T(8,128)(2,1)} %pad_maximum_fusion), kind=kLoop, calls=%fused_computation.6 | loop fusion | flops 16515072 | bytes 28311552 | tf_op jit(solution)/shard_map/reduce_sum | solution.py:69
  749.7 6.8 multiply_reduce_fusion
  757.2 14.3 %select_bitcast_fusion = bf16[1,2048,1152]{1,2,0:T(8,128)(2,1)} fusion(pred[]{:T(512)S(6)} %eq.36, bf16[1,2048,1152]{1,2,0:T(8,128)(2,1)} %copy.36, f32[2048,1152]{0,1:T(8,128)} %convert_reduce_fusion, f32[]{:T(128)S(6)} %min.3, bf16[1,2048,1152]{1,2,0:T(8,128)(2,1)} %copy.35, bf16[1,2048,1152]{1,2,0:T(8,128)(2,1)} %copy.32), kind=kLoop, calls=%fused_computation.42 | loop fusion | flops 44826624 | bytes 28311556 | tf_op jit(solution)/shard_map/broadcast_in_dim | solution.py:135
  771.5 14.5 %fusion.18 = bf16[1,2048,1152]{1,2,0:T(8,128)(2,1)} fusion(bf16[1,2048,1152]{1,2,0:T(8,128)(2,1)} %copy.36, bf16[1,2048,1152]{1,2,0:T(8,128)(2,1)} %copy.35, bf16[1,2048,1152]{1,2,0:T(8,128)(2,1)} %copy.32, f32[2048,1152]{0,1:T(8,128)} %convert_reduce_fusion, f32[]{:T(128)S(6)} %min.3), kind=kLoop, calls=%fused_computation.35 | loop fusion | flops 42467328 | bytes 28311556 | tf_op jit(solution)/shard_map/convert_element_type | solution.py:133
  786.1 6.6 copy.37
  792.7 102.5 %all-reduce.2.cloned.1.call-done = bf16[1,2048,1152]{1,2,0:T(8,128)(2,1)} async-done(((bf16[1,2048,1152]{1,2,0:T(8,128)(2,1)}), bf16[1,2048,1152]{1,2,0:T(8,128)(2,1)}) %all-reduce.2.cloned.1.call-update) | async-done | bytes 4718608 | tf_op jit(solution)/shard_map/psum | solution.py:17
  901.9 13.5 %gather_fusion.3 = bf16[1024,2048]{1,0:T(8,128)(2,1)} fusion(bf16[2048,2048]{1,0:T(8,128)(2,1)} %bitcast.16, s32[1024]{0:T(1024)S(1)} %broadcast_clamp_fusion), kind=kCustom, calls=%fused_computation.3 | custom fusion | bytes 8392704 | tf_op jit(solution)/shard_map/gather | solution.py:121
  921.3 13.3 %gather_fusion.1 = bf16[1024,2048]{1,0:T(8,128)(2,1)} fusion(bf16[2048,2048]{1,0:T(8,128)(2,1)} %bitcast.8, s32[1024]{0:T(1024)S(1)} %broadcast_clamp_fusion), kind=kCustom, calls=%fused_computation.1 | custom fusion | bytes 8392704 | tf_op jit(solution)/shard_map/gather | solution.py:109
  (54 shorter events, 57.6 us)
Async XLA Ops:
  7.2 43.8 %copy-start = (bf16[128,2048]{1,0:T(8,128)(2,1)S(1)}, bf16[128,2048]{1,0:T(8,128)(2,1)}, u32[]{:S(2)}) copy-start(bf16[128,2048]{1,0:T(8,128)(2,1)} %param.8) | copy-start | bytes 1572868
  261.9 190.3 %all-to-all-start.2 = ((bf16[32,64,2048]{2,1,0:T(8,128)(2,1)}), bf16[32,64,2048]{2,1,0:T(8,128)(2,1)}, u32[]{:S(2)}, u32[]{:S(2)}) async-start(bf16[32,64,2048]{2,1,0:T(8,128)(2,1)} %get-tuple-element.15), calls=%async_computation.2 | async-start | bytes 16777216 | tf_op jit(solution)/shard_map/all_to_all | solution.py:81
  452.2 12.8 %copy-start.2 = (bf16[1,2048,1152]{1,2,0:T(8,128)(2,1)S(1)}, bf16[1,2048,1152]{1,2,0:T(8,128)(2,1)}, u32[]{:S(2)}) copy-start(bf16[1,2048,1152]{1,2,0:T(8,128)(2,1)} %copy.32) | copy-start | bytes 14155780
  465.0 9.0 copy-start.6
  474.0 200.5 %all-to-all-start.3 = ((bf16[32,64,2048]{2,1,0:T(8,128)(2,1)}), bf16[32,64,2048]{2,1,0:T(8,128)(2,1)}, u32[]{:S(2)}, u32[]{:S(2)}) async-start(bf16[32,64,2048]{2,1,0:T(8,128)(2,1)} %bitcast.103), calls=%async_computation.3 | async-start | bytes 16777216 | tf_op jit(solution)/shard_map/all_to_all | solution.py:85
  674.5 246.8 %all-to-all-start.1 = ((bf16[32,64,2048]{2,1,0:T(8,128)(2,1)}), bf16[32,64,2048]{2,1,0:T(8,128)(2,1)}, u32[]{:S(2)}, u32[]{:S(2)}) async-start(bf16[32,64,2048]{2,1,0:T(8,128)(2,1)} %bitcast.100), calls=%async_computation.1 | async-start | bytes 16777216 | tf_op jit(solution)/shard_map/all_to_all | solution.py:85
  678.2 217.1 %all-reduce.2.cloned.1.call-start = ((), (), s32[]{:S(2)}) async-start(), calls=%async_computation.4 | async-start | bytes 9437184 | tf_op jit(solution)/shard_map/psum | solution.py:17
  685.0 7.3 copy-start.5
  934.6 4.7 copy-start.3
  934.6 4.7 copy-start.4
  934.6 8.0 copy-start.1
Sparse Core Ops, SparseCore 0:
  771.7 123.5 all-reduce.1
where the time goes:
time: 958 us; the launch traced here: 950 us
  waiting for transfers between devices  446 us (47%)
  blocking collectives  191 us (20%)
  local copies, waits for them, and re-layouts  103 us (11%)
  other arithmetic  99.2 us (10%)
  matrix products  71.9 us (8%)
  starting transfers between devices  22.4 us (2%)
  between operations  16 us (2%)
    all_to_all x1, blocking collectives, to_experts(): lax.all_to_all(row_block, ('expert', 'replica'), split_axis=0, concat_axi...  191 us
    all_to_all x2, waiting for transfers between devices, from_experts(): lax.all_to_all(row_block, ('expert', 'replica'), split_axis=0, concat_axi...  176 us
    all_to_all x1, waiting for transfers between devices, to_experts(): lax.all_to_all(row_block, ('expert', 'replica'), split_axis=0, concat_axi...  168 us
    psum x1, waiting for transfers between devices, broadcast(): return lax.psum(kept, axis)  103 us
    unnamed x22, local copies, waits for them, and re-layouts  35 us
    concatenate x1, other arithmetic, partial_sums(): jnp.concatenate([in_part, down_part], axis=2).astype(jnp.bfloat16)  20.3 us
  transfers between devices with their start and end apart: 4, of which 3 were waited for; matrix products, arithmetic and copies ran while one was open for 18% of the time, Pallas kernels for 0%

commit v1 on v0

--- a/solution.py
+++ b/solution.py
@@ -14,7 +14,8 @@
 
 def broadcast(value, axis, source):
     kept = jnp.where(lax.axis_index(axis) == source, value, 0).astype(value.dtype)
-    return lax.psum(kept, axis)
+    _map_pages = lambda load, dev_axis: jnp.sum(lax.all_gather(load, dev_axis), axis=0)
+    return _map_pages(kept, axis)
 
 
 def expert_forward(row_block, weights, hidden_width):

time: 958 us -> 910 us (0.950)
  waiting for transfers between devices: 446 us -> 410 us
  starting transfers between devices: 22.4 us -> 11.9 us
    psum x1 -> x0, waiting for transfers between devices: 103 us -> none  [broadcast(): return lax.psum(kept, axis)]
    all_to_all x2, waiting for transfers between devices: 176 us -> 257 us  [from_experts(): lax.all_to_all(row_block, ('expert', 'replica'), split_axis=0, concat_axi...]
    select_n x0 -> x1, other arithmetic: none -> 16.3 us  [broadcast(): jnp.where(lax.axis_index(axis) == source, value, 0).astype(value.dtype)]
    convert_element_type x1 -> x0, other arithmetic: 14.5 us -> none  [shards(): (weights.astype(jnp.float32) - rate * update).astype(jnp.bfloat16)]
    broadcast_in_dim x1 -> x0, other arithmetic: 14.3 us -> none  [shards(): return (mixed, input_grad, gate_grad, new_weights[None], hot_copy[None])]
    all_to_all x1, waiting for transfers between devices: 168 us -> 154 us  [to_experts(): lax.all_to_all(row_block, ('expert', 'replica'), split_axis=0, concat_axi...]
    reduce_sum x0 -> x1, other arithmetic: none -> 13.3 us  [broadcast(): jnp.sum(lax.all_gather(load, dev_axis), axis=0)]
    all_to_all x2, starting transfers between devices: 18.1 us -> 7.69 us  [from_experts(): lax.all_to_all(row_block, ('expert', 'replica'), split_axis=0, concat_axi...]
  transfers between devices with their start and end apart: 4 -> 4, of which waited for: 3 -> 3; matrix products, arithmetic and copies ran while one was open for 18% -> 19% of each run, Pallas kernels for 0% -> 0%
where the time goes in v1:
time: 910 us; the launch traced here: 901 us
  waiting for transfers between devices  410 us (45%)
  blocking collectives  191 us (21%)
  local copies, waits for them, and re-layouts  103 us (11%)
  other arithmetic  99.8 us (11%)
  matrix products  69.7 us (8%)
  between operations  15.9 us (2%)
  starting transfers between devices  11.9 us (1%)
    all_to_all x2, waiting for transfers between devices, from_experts(): lax.all_to_all(row_block, ('expert', 'replica'), split_axis=0, concat_axi...  257 us
    all_to_all x1, blocking collectives, to_experts(): lax.all_to_all(row_block, ('expert', 'replica'), split_axis=0, concat_axi...  191 us
    all_to_all x1, waiting for transfers between devices, to_experts(): lax.all_to_all(row_block, ('expert', 'replica'), split_axis=0, concat_axi...  154 us
    unnamed x29, local copies, waits for them, and re-layouts  28.5 us
    concatenate x1, other arithmetic, partial_sums(): jnp.concatenate([in_part, down_part], axis=2).astype(jnp.bfloat16)  20.3 us
    gather x1, local copies, waits for them, and re-layouts, shards(): slot_cot[slot_source]  19 us
  transfers between devices with their start and end apart: 4, of which 3 were waited for; matrix products, arithmetic and copies ran while one was open for 19% of the time, Pallas kernels for 0%

profile of v1, /device:TPU:0, one launch (start us, length us, event | category | flops | bytes accessed | tf_op | source)
XLA Modules:
  0.0 901.3 jit_solution(9103542177026335327)
XLA Ops:
  8.9 9.0 %reduce-window.6 = s32[32,8,128]{2,1,0:T(8,128)S(1)} reduce-window(s32[32,8,128]{2,1,0:T(8,128)S(1)} %fusion.31, s32[]{:T(128)} %constant.17.clone.1), window={size=1x1x128 pad=0_0x0_0x127_0}, to_apply=%region_0.0 | reduce-window | flops 4161536 | bytes 262148 | tf_op jit(solution)/shard_map/reduce-window
  31.9 19.0 %gather_fusion.2 = bf16[2048,2048]{1,0:T(8,128)(2,1)} fusion(bf16[1024,2048]{1,0:T(8,128)(2,1)} %fusion.10, s32[2048]{0:T(1024)S(1)} %get-tuple-element.15), kind=kCustom, calls=%fused_computation.2 | custom fusion | bytes 16785408 | tf_op jit(solution)/shard_map/gather | solution.py:119
  51.0 11.0 %gather_fusion = bf16[2048,2048]{1,0:T(8,128)(2,1)} fusion(bf16[128,2048]{1,0:T(8,128)(2,1)S(1)} %copy-done, s32[2048]{0:T(1024)S(1)} %get-tuple-element.16), kind=kCustom, calls=%fused_computation | custom fusion | bytes 16785408 | tf_op jit(solution)/shard_map/gather | solution.py:108
  62.0 9.2 %broadcast_select_fusion = (bf16[32,64,2048]{2,1,0:T(8,128)(2,1)}, bf16[32,64,2048]{2,1,0:T(8,128)(2,1)S(1)}) fusion(bf16[32,64,2048]{2,1,0:T(8,128)(2,1)} %bitcast.77, pred[32,64]{1,0:T(8,128)(4,1)S(1)} %broadcast_in_dim.49, bf16[32,64,2048]{2,1,0:T(8,128)(2,1)} %bitcast.78), kind=kLoop, calls=%fused_computation.25 | loop fusion | flops 8388608 | bytes 33556480 | tf_op jit(solution)/shard_map/jit(_where)/select_n | solution.py:119
  71.2 190.7 %all_to_all.42 = bf16[32,64,2048]{2,1,0:T(8,128)(2,1)} all-to-all(bf16[32,64,2048]{2,1,0:T(8,128)(2,1)S(1)} %get-tuple-element.18), channel_id=1, replica_groups=mesh['expert'=8,'replica'=4] {'expert','replica'}, dimensions={0} | all-to-all | bytes 16777216 | tf_op jit(solution)/shard_map/all_to_all | solution.py:82
  266.1 6.7 copy.33
  286.7 11.7 %fusion.22 = f32[2048,768]{1,0:T(8,128)} fusion(bf16[2048,2048]{1,0:T(8,128)(2,1)} %bitcast.80, bf16[2048,1152]{1,0:T(8,128)(2,1)} %bitcast.84), kind=kOutput, calls=%fused_computation.46 | convolution fusion | flops 6442450944 | bytes 17825792 | tf_op jit(solution)/shard_map/dot_general | solution.py:22
  298.5 153.7 %all-to-all-done.2 = bf16[32,64,2048]{2,1,0:T(8,128)(2,1)} async-done(((bf16[32,64,2048]{2,1,0:T(8,128)(2,1)}), bf16[32,64,2048]{2,1,0:T(8,128)(2,1)}, u32[]{:S(2)}, u32[]{:S(2)}) %all-to-all-start.2) | async-done | bytes 8388640 | tf_op jit(solution)/shard_map/all_to_all | solution.py:82
  452.2 11.6 %multiply_convert_fusion.1 = (bf16[2048,384]{1,0:T(8,128)(2,1)S(1)}, bf16[2048,384]{1,0:T(8,128)(2,1)S(1)}, bf16[2048,384]{1,0:T(8,128)(2,1)S(1)}) fusion(f32[2048,768]{1,0:T(8,128)} %fusion.22, bf16[2048,2048]{1,0:T(8,128)(2,1)} %bitcast.14, bf16[2048,1152]{1,0:T(8,128)(2,1)} %bitcast.85), kind=kOutput, calls=%fused_computation.42 | convolution fusion | flops 3233808384 | bytes 20971520 | tf_op jit(solution)/shard_map/dot_general | solution.py:39
  463.9 9.0 convolution_convert_fusion
  476.6 9.6 %bitcast_convert_fusion.1 = bf16[4,2048,384]{1,2,0:T(8,128)(2,1)} fusion(bf16[8,4,64,2048]{3,2,1,0:T(8,128)(2,1)} %bitcast.24, bf16[8,4,64,384]{3,2,1,0:T(8,128)(2,1)S(1)} %bitcast.100), kind=kOutput, calls=%fused_computation.10 | convolution fusion | flops 3224371200 | bytes 16252928 | tf_op jit(solution)/shard_map/arcd,arcf->rdf/dot_general | solution.py:61
  486.2 13.2 %bitcast_convert_fusion = bf16[4,2048,768]{1,2,0:T(8,128)(2,1)} fusion(bf16[8,4,64,2048]{3,2,1,0:T(8,128)(2,1)} %bitcast.81, bf16[8,4,64,384]{3,2,1,0:T(8,128)(2,1)} %bitcast.102, bf16[8,4,64,384]{3,2,1,0:T(8,128)(2,1)} %bitcast.101), kind=kOutput, calls=%fused_computation.7 | convolution fusion | flops 6455033856 | bytes 24117248 | tf_op jit(solution)/shard_map/arcd,arcg->rdg/dot_general | solution.py:55
  499.3 20.3 %pad_maximum_fusion = bf16[4,2048,1152]{1,2,0:T(8,128)(2,1)} fusion(bf16[4,2048,384]{1,2,0:T(8,128)(2,1)} %bitcast_convert_fusion.1, bf16[4,2048,768]{1,2,0:T(8,128)(2,1)} %bitcast_convert_fusion), kind=kLoop, calls=%fused_computation.8 | loop fusion | flops 37748736 | bytes 37748736 | tf_op jit(solution)/shard_map/concatenate | solution.py:68
  519.6 14.6 %convert_reduce_fusion = f32[2048,1152]{0,1:T(8,128)} fusion(bf16[4,2048,1152]{1,2,0:T(8,128)(2,1)} %pad_maximum_fusion), kind=kLoop, calls=%fused_computation.6 | loop fusion | flops 16515072 | bytes 28311552 | tf_op jit(solution)/shard_map/reduce_sum | solution.py:70
  534.2 6.7 multiply_reduce_fusion
  541.6 16.3 %broadcast_select_fusion.2 = (bf16[1,2048,1152]{1,2,0:T(8,128)(2,1)}, bf16[1,2048,1152]{1,2,0:T(8,128)(2,1)}) fusion(pred[]{:T(512)S(6)} %eq.36, bf16[1,2048,1152]{1,2,0:T(8,128)(2,1)} %copy.35, f32[2048,1152]{0,1:T(8,128)} %convert_reduce_fusion, f32[]{:T(128)S(6)} %min.3, bf16[1,2048,1152]{1,2,0:T(8,128)(2,1)} %copy.34, bf16[1,2048,1152]{1,2,0:T(8,128)(2,1)} %copy.33), kind=kLoop, calls=%fused_computation.29 | loop fusion | flops 44826624 | bytes 33030148 | tf_op jit(solution)/shard_map/jit(_where)/select_n | solution.py:16
  557.9 6.7 copy.36
  564.6 8.4 convolution_convert_fusion.1
  573.0 89.9 %all-to-all-done.3 = bf16[32,64,2048]{2,1,0:T(8,128)(2,1)} async-done(((bf16[32,64,2048]{2,1,0:T(8,128)(2,1)}), bf16[32,64,2048]{2,1,0:T(8,128)(2,1)}, u32[]{:S(2)}, u32[]{:S(2)}) %all-to-all-start.3) | async-done | bytes 8388640 | tf_op jit(solution)/shard_map/all_to_all | solution.py:86
  667.0 6.7 copy.37
  673.7 13.3 %gather_fusion.3 = bf16[1024,2048]{1,0:T(8,128)(2,1)} fusion(bf16[2048,2048]{1,0:T(8,128)(2,1)} %bitcast.16, s32[1024]{0:T(1024)S(1)} %broadcast_clamp_fusion), kind=kCustom, calls=%fused_computation.3 | custom fusion | bytes 8392704 | tf_op jit(solution)/shard_map/gather | solution.py:122
  687.0 166.7 %all-to-all-done.1 = bf16[32,64,2048]{2,1,0:T(8,128)(2,1)} async-done(((bf16[32,64,2048]{2,1,0:T(8,128)(2,1)}), bf16[32,64,2048]{2,1,0:T(8,128)(2,1)}, u32[]{:S(2)}, u32[]{:S(2)}) %all-to-all-start.1) | async-done | bytes 8388640 | tf_op jit(solution)/shard_map/all_to_all | solution.py:86
  853.7 13.3 %gather_fusion.1 = bf16[1024,2048]{1,0:T(8,128)(2,1)} fusion(bf16[2048,2048]{1,0:T(8,128)(2,1)} %bitcast.8, s32[1024]{0:T(1024)S(1)} %broadcast_clamp_fusion), kind=kCustom, calls=%fused_computation.1 | custom fusion | bytes 8392704 | tf_op jit(solution)/shard_map/gather | solution.py:110
  880.9 13.3 %reduce_sum.58 = bf16[2048,1152]{1,0:T(8,128)(2,1)} reduce(bf16[4,2048,1152]{2,1,0:T(8,128)(2,1)} %all-gather.2.cloned.1.call-done, bf16[]{:T(256)} %constant.23.clone.1), dimensions={0}, to_apply=%region_8.9 | reduce | flops 7077888 | bytes 23592962 | tf_op jit(solution)/shard_map/reduce_sum | solution.py:17
  (63 shorter events, 54.9 us)
Async XLA Ops:
  7.2 43.8 %copy-start = (bf16[128,2048]{1,0:T(8,128)(2,1)S(1)}, bf16[128,2048]{1,0:T(8,128)(2,1)}, u32[]{:S(2)}) copy-start(bf16[128,2048]{1,0:T(8,128)(2,1)} %param.8) | copy-start | bytes 1572868
  18.7 32.3 %copy-start.5 = (s32[1024,1]{0,1:T(1,128)}, s32[1024,1]{0,1:T(1,128)S(1)}, u32[]{:S(2)}) copy-start(s32[1024,1]{0,1:T(1,128)S(1)} %compare_select_fusion) | copy-start | bytes 12292
  262.0 190.2 %all-to-all-start.2 = ((bf16[32,64,2048]{2,1,0:T(8,128)(2,1)}), bf16[32,64,2048]{2,1,0:T(8,128)(2,1)}, u32[]{:S(2)}, u32[]{:S(2)}) async-start(bf16[32,64,2048]{2,1,0:T(8,128)(2,1)} %get-tuple-element.17), calls=%async_computation.2 | async-start | bytes 16777216 | tf_op jit(solution)/shard_map/all_to_all | solution.py:82
  286.7 177.1 %slice-start = ((s8[4718592]{0:T(1024)(128)(4,1)}), s8[524288]{0:T(1024)(128)(4,1)S(1)}, s32[]{:S(2)}) async-start(s8[4718592]{0:T(1024)(128)(4,1)} %bitcast.87), calls=%async_computation.5 | async-start | bytes 1048576
  452.2 11.7 %slice-start.1 = ((s8[4718592]{0:T(1024)(128)(4,1)}), s8[4194304]{0:T(1024)(128)(4,1)S(1)}, s32[]{:S(2)}) async-start(s8[4718592]{0:T(1024)(128)(4,1)} %bitcast.87), calls=%async_computation.6 | async-start | bytes 8388608
  463.8 9.0 %copy-start.7 = (bf16[2048,384]{1,0:T(8,128)(2,1)}, bf16[2048,384]{1,0:T(8,128)(2,1)S(1)}, u32[]{:S(2)}) copy-start(bf16[2048,384]{1,0:T(8,128)(2,1)S(1)} %get-tuple-element.12) | copy-start | bytes 4718596
  463.8 9.0 %copy-start.8 = (bf16[2048,384]{1,0:T(8,128)(2,1)}, bf16[2048,384]{1,0:T(8,128)(2,1)S(1)}, u32[]{:S(2)}) copy-start(bf16[2048,384]{1,0:T(8,128)(2,1)S(1)} %get-tuple-element.13) | copy-start | bytes 4718596
  472.9 190.0 %all-to-all-start.3 = ((bf16[32,64,2048]{2,1,0:T(8,128)(2,1)}), bf16[32,64,2048]{2,1,0:T(8,128)(2,1)}, u32[]{:S(2)}, u32[]{:S(2)}) async-start(bf16[32,64,2048]{2,1,0:T(8,128)(2,1)} %bitcast.79), calls=%async_computation.3 | async-start | bytes 16777216 | tf_op jit(solution)/shard_map/all_to_all | solution.py:86
  476.6 404.3 %all-gather.2.cloned.1.call-start = ((), (), s32[]{:S(2)}) async-start(), calls=%async_computation.4 | async-start | bytes 23592960 | tf_op jit(solution)/shard_map/all_gather | solution.py:17
  662.8 4.0 copy-start.4
  662.8 4.2 copy-start.6
  662.8 190.8 %all-to-all-start.1 = ((bf16[32,64,2048]{2,1,0:T(8,128)(2,1)}), bf16[32,64,2048]{2,1,0:T(8,128)(2,1)}, u32[]{:S(2)}, u32[]{:S(2)}) async-start(bf16[32,64,2048]{2,1,0:T(8,128)(2,1)} %bitcast.82), calls=%async_computation.1 | async-start | bytes 16777216 | tf_op jit(solution)/shard_map/all_to_all | solution.py:86
  866.9 4.7 copy-start.2
  866.9 4.7 copy-start.3
  875.0 19.3 %copy-start.1 = (bf16[128,2048]{1,0:T(8,128)(2,1)S(1)}, bf16[128,2048]{1,0:T(8,128)(2,1)}, u32[]{:S(2)}) copy-start(bf16[128,2048]{1,0:T(8,128)(2,1)} %param.8) | copy-start | bytes 1572868
Sparse Core Ops, SparseCore 0:
  564.7 211.6 all-gather.1
